TPU v7x, 32 devices: a whole 2x2x4 slice. The times are simulated.
32 devices in a mesh: grp: 4 (over y, x), lm: 8 (over z, core).
Axes of the slice: x: 2, y: 2, z: 4, core: 2. Of those that a mesh axis runs over, the one named last changes fastest.
Arguments:
- embeddings: bfloat16 [8192, 512], P(('grp', 'lm')), may hold values from -14 to 14
- landmarks: bfloat16 [16384, 512], P('lm'), may hold values from -14 to 14
- start_vectors: float32 [8192, 128], P(('grp', 'lm')), may hold values from -10 to 10
- row_weight: float32 [8192], P(('grp', 'lm')), may hold values from 0.1 to 9
- spread: float32 [1], replicated, may hold values from 11.313708 to 33.941124
Outputs:
- subspace: float32 [8192, 128], P(('grp', 'lm'))
All inputs are finite; a program needn't handle non-finite values.
Results may differ from a plain program's by a relative error of at most 0.019.
Values may be sent and summed in bfloat16 or wider, within the bound.
A program may use at most 128 MiB of HBM per device.

v0:
```python
import jax
import jax.numpy as jnp
from jax import lax
from jax.sharding import PartitionSpec as P

ITERS = 2


def unit_rows(values):
    values = values.astype(jnp.float32)
    scale = lax.rsqrt(jnp.sum(values * values, axis=1, keepdims=True) + 1e-06)
    return (values * scale).astype(jnp.bfloat16)


def kernel_values(rows_unit, marks_unit, gamma):
    cosine = jnp.einsum("rd,ld->rl", rows_unit, marks_unit, preferred_element_type=jnp.float32)
    return jnp.exp(gamma * cosine)


def local(embeddings, landmarks, start_vectors, row_weight, spread):
    own_rows = embeddings.shape[0]
    marks = landmarks.shape[0]
    groups = lax.axis_size("grp")
    members = lax.axis_size("lm")
    total_rows = own_rows * groups * members
    group_rows = own_rows * members
    gamma = spread[0]
    rows_unit = unit_rows(embeddings)
    marks_unit = unit_rows(landmarks)
    sums = jnp.zeros((marks,), jnp.float32)
    weights = jnp.zeros((group_rows,), jnp.float32)
    part_rows = lax.all_gather(rows_unit, "lm", axis=0, tiled=True)
    part_weight = lax.all_gather(row_weight.astype(jnp.bfloat16), "lm", axis=0, tiled=True).astype(
        jnp.float32
    )
    values = kernel_values(part_rows, marks_unit, gamma)
    build_tile = values.astype(jnp.bfloat16)
    weights = lax.dynamic_update_slice_in_dim(weights, part_weight, jnp.int32(0), 0)
    sums = sums + jnp.sum(part_weight[:, None] * values, axis=0)
    mean_sum, weight_sum = lax.psum((sums, jnp.sum(weights)), "grp")
    means = mean_sum / weight_sum
    vectors = start_vectors
    weighted_full = row_weight[:, None] * vectors
    totals = lax.psum(jnp.sum(weighted_full, axis=0), ("grp", "lm"))
    group_weighted = lax.all_gather(weighted_full.astype(jnp.bfloat16), "lm", axis=0, tiled=True)
    for step in range(ITERS):
        side = (
            lax.psum(
                jnp.einsum(
                    "rl,rv->lv", build_tile, group_weighted, preferred_element_type=jnp.float32
                ),
                "grp",
            )
            - means[:, None] * totals[None, :]
        )
        side_b = side.astype(jnp.bfloat16)
        shift = jnp.dot(means, side_b.astype(jnp.float32), precision=lax.Precision.HIGHEST)
        partial_rows = weights[:, None] * (
            jnp.dot(build_tile, side_b, preferred_element_type=jnp.float32) - shift[None, :]
        )
        image = lax.psum(partial_rows, "lm")
        square, column = lax.psum(
            (jnp.sum(image * image, axis=0), jnp.sum(weights[:, None] * image, axis=0)), "grp"
        )
        scale = jnp.sqrt(square / total_rows + 1e-06)
        group_vectors = image / scale[None, :]
        totals = column / scale
        group_weighted = (weights[:, None] * group_vectors).astype(jnp.bfloat16)
        vectors = lax.dynamic_slice_in_dim(
            group_vectors, lax.axis_index("lm") * own_rows, own_rows, 0
        )
    return vectors


def solution(mesh):
    in_specs = (
        P(("grp", "lm"), None),
        P("lm", None),
        P(("grp", "lm"), None),
        P(("grp", "lm")),
        P(),
    )
    out_specs = P(("grp", "lm"), None)
    return jax.shard_map(local, mesh=mesh, in_specs=in_specs, out_specs=out_specs, check_vma=False)
```

profile of v0, /device:TPU:0, one launch (start us, length us, event | category | flops | bytes accessed | tf_op | source)
XLA Modules:
  0.0 337.8 jit_solution(3544346859675565320)
XLA Ops:
  6.5 1.1 fusion.8
  7.6 1.8 fusion.9
  9.4 0.0 all-reduce.7.cloned.1.call-start
  9.5 0.7 convert_element_type.35
  10.2 13.5 %all-gather = bf16[8,1,256]{2,1,0:T(2,128)(2,1)S(1)} all-gather(bf16[1,1,256]{2,1,0:T(2,128)(2,1)S(1)} %reshape.21), channel_id=1, replica_groups=mesh['grp'=4,'lm'=8] {'lm'}, dimensions={0}, use_global_device_ids=true | all-gather | bytes 4608 | tf_op jit(solution)/shard_map/all_gather | solution.py:33
  24.3 2.1 fusion.1
  26.4 1.0 multiply_reduce_fusion.4
  27.4 17.3 %all_gather.11 = bf16[2048,128]{1,0:T(8,128)(2,1)S(1)} all-gather(bf16[256,128]{1,0:T(8,128)(2,1)S(1)} %get-tuple-element.14), channel_id=1, replica_groups=mesh['grp'=4,'lm'=8] {'lm'}, dimensions={0}, use_global_device_ids=true | all-gather | bytes 589824 | tf_op jit(solution)/shard_map/all_gather | solution.py:45
  44.7 1.0 all-gather.3.cloned.1.call-done
  45.7 7.8 %multiply_reduce_fusion = (f32[2048]{0:T(1024)S(1)}, bf16[2048,2048]{1,0:T(8,128)(2,1)S(1)}) fusion(f32[2048]{0:T(1024)S(1)} %bitcast.19, f32[]{:T(128)} %bitcast.16, bf16[2048,512]{1,0:T(8,128)(2,1)} %all-gather.3.cloned.1.call-done, bf16[2048,512]{1,0:T(8,128)(2,1)} %param.6, f32[2048]{0:T(1024)S(1)} %add_rsqrt_fusion), kind=kOutput, calls=%fused_computation | convolution fusion | flops 4314888192 | bytes 12607492 | tf_op jit(solution)/shard_map/rd,ld->rl/dot_general | solution.py:16
  53.5 3.2 copy-done
  56.7 3.4 %fusion.14 = f32[2048,128]{1,0:T(8,128)} fusion(bf16[2048,2048]{1,0:T(8,128)(2,1)S(1)} %get-tuple-element.12, bf16[2048,128]{1,0:T(8,128)(2,1)S(1)} %all_gather.11), kind=kOutput, calls=%fused_computation.38 | convolution fusion | flops 1073741824 | bytes 9961472 | tf_op jit(solution)/shard_map/rl,rv->lv/dot_general | solution.py:49
  60.2 0.0 all-reduce.9.cloned.1.call-start
  60.2 40.3 %psum.73 = f32[128]{0:T(128)S(1)} all-reduce(f32[128]{0:T(128)S(1)} %get-tuple-element.13), channel_id=1, replica_groups=mesh['grp'=4,'lm'=8] {'grp','lm'}, use_global_device_ids=true, to_apply=%region_8.0 | all-reduce | flops 128 | bytes 1024 | tf_op jit(solution)/shard_map/psum | solution.py:44
  100.5 0.6 convert_reduce_fusion
  101.1 11.7 %all-reduce.1 = (f32[2048]{0:T(1024)S(1)}, f32[]{:T(128)}) all-reduce(f32[2048]{0:T(1024)S(1)} %get-tuple-element.11, f32[]{:T(128)} %convert_reduce_fusion), channel_id=1, replica_groups=mesh['grp'=4,'lm'=8] {'grp'}, use_global_device_ids=true, to_apply=%region_4.0 | all-reduce | flops 2049 | bytes 16392 | tf_op jit(solution)/shard_map/psum | solution.py:40
  112.8 0.6 broadcast_divide_fusion
  113.5 1.8 convolution_bitcast_fusion.1
  115.3 7.1 %fusion.4 = f32[2048,128]{1,0:T(8,128)} fusion(bf16[2048,2048]{1,0:T(8,128)(2,1)} %copy-done, f32[128]{0:T(128)S(1)} %convolution_bitcast_fusion.1, f32[2048]{0:T(1024)S(1)} %bitcast.20, f32[2048,128]{1,0:T(8,128)} %all-reduce.7.cloned.1.call-done, f32[128]{0:T(128)S(1)} %psum.73, f32[2048]{0:T(1024)S(1)} %broadcast_divide_fusion), kind=kOutput, calls=%fused_computation.10 | convolution fusion | flops 1075052544 | bytes 10503168 | tf_op jit(solution)/shard_map/dot_general | solution.py:59
  122.4 0.0 all-reduce.11.cloned.1.call-start
  122.5 58.7 %all-reduce.9.cloned.1.call-done = f32[2048,128]{1,0:T(8,128)} async-done(((f32[2048,128]{1,0:T(8,128)}), f32[2048,128]{1,0:T(8,128)}) %all-reduce.9.cloned.1.call-update) | async-done | bytes 1048592 | tf_op jit(solution)/shard_map/psum | solution.py:61
  181.1 1.6 multiply_reduce_fusion.2
  182.7 10.0 %all-reduce = (f32[128]{0:T(128)S(1)}, f32[128]{0:T(128)S(1)}) all-reduce(f32[128]{0:T(128)S(1)} %get-tuple-element.6, f32[128]{0:T(128)S(1)} %get-tuple-element.5), channel_id=1, replica_groups=mesh['grp'=4,'lm'=8] {'grp'}, use_global_device_ids=true, to_apply=%region_11.0 | all-reduce | flops 256 | bytes 2048 | tf_op jit(solution)/shard_map/psum | solution.py:62
  192.7 7.3 %fusion.10 = f32[2048,128]{1,0:T(8,128)} fusion(bf16[2048,2048]{1,0:T(8,128)(2,1)} %copy-done, f32[2048,128]{1,0:T(8,128)} %all-reduce.9.cloned.1.call-done, f32[128]{0:T(128)S(1)} %get-tuple-element.16, f32[2048]{0:T(1024)S(1)} %bitcast.22), kind=kOutput, calls=%fused_computation.25 | convolution fusion | flops 1074528256 | bytes 10494464 | tf_op jit(solution)/shard_map/rl,rv->lv/dot_general | solution.py:49
  200.0 0.0 all-reduce.13.cloned.1.call-start
  200.1 49.9 %all-reduce.11.cloned.1.call-done = f32[2048,128]{1,0:T(8,128)} async-done(((f32[2048,128]{1,0:T(8,128)}), f32[2048,128]{1,0:T(8,128)}) %all-reduce.11.cloned.1.call-update) | async-done | bytes 1048592 | tf_op jit(solution)/shard_map/psum | solution.py:48
  250.0 1.8 convolution_bitcast_fusion
  251.8 7.1 %fusion.3 = f32[2048,128]{1,0:T(8,128)} fusion(bf16[2048,2048]{1,0:T(8,128)(2,1)} %copy-done, f32[128]{0:T(128)S(1)} %convolution_bitcast_fusion, f32[2048]{0:T(1024)S(1)} %bitcast.23, f32[2048,128]{1,0:T(8,128)} %all-reduce.11.cloned.1.call-done, f32[128]{0:T(128)S(1)} %get-tuple-element.15, f32[2048]{0:T(1024)S(1)} %broadcast_divide_fusion), kind=kOutput, calls=%fused_computation.8 | convolution fusion | flops 1075052544 | bytes 10503168 | tf_op jit(solution)/shard_map/dot_general | solution.py:59
  258.9 59.5 %all-reduce.13.cloned.1.call-done = f32[2048,128]{1,0:T(8,128)} async-done(((f32[2048,128]{1,0:T(8,128)}), f32[2048,128]{1,0:T(8,128)}) %all-reduce.13.cloned.1.call-update) | async-done | bytes 1048592 | tf_op jit(solution)/shard_map/psum | solution.py:61
  318.4 1.5 multiply_reduce_fusion.1
  319.9 9.8 %psum.79 = f32[128]{0:T(128)S(1)} all-reduce(f32[128]{0:T(128)S(1)} %multiply_reduce_fusion.1), channel_id=1, replica_groups=mesh['grp'=4,'lm'=8] {'grp'}, use_global_device_ids=true, to_apply=%region_17.0 | all-reduce | flops 128 | bytes 1024 | tf_op jit(solution)/shard_map/psum | solution.py:62
  329.7 1.6 dynamic-slice_divide_fusion
  (14 shorter events, 0.2 us)
Async XLA Ops:
  6.5 39.1 %all-gather.3.cloned.1.call-start = ((), (), s32[]{:S(2)}) async-start(), calls=%async_computation | async-start | bytes 2359296 | tf_op jit(solution)/shard_map/all_gather | solution.py:32
  9.4 104.1 %all-reduce.7.cloned.1.call-start = ((), (), s32[]{:S(2)}) async-start(), calls=%async_computation.1 | async-start | bytes 2097152 | tf_op jit(solution)/shard_map/psum | solution.py:48
  53.5 3.2 copy-start
  60.2 120.9 %all-reduce.9.cloned.1.call-start = ((), (), s32[]{:S(2)}) async-start(), calls=%async_computation.2 | async-start | bytes 2097152 | tf_op jit(solution)/shard_map/psum | solution.py:61
  122.4 127.6 %all-reduce.11.cloned.1.call-start = ((), (), s32[]{:S(2)}) async-start(), calls=%async_computation.3 | async-start | bytes 2097152 | tf_op jit(solution)/shard_map/psum | solution.py:48
  200.0 118.3 %all-reduce.13.cloned.1.call-start = ((), (), s32[]{:S(2)}) async-start(), calls=%async_computation.4 | async-start | bytes 2097152 | tf_op jit(solution)/shard_map/psum | solution.py:61
Sparse Core Ops, SparseCore 0:
  9.6 36.0 all-gather.2
  60.3 52.8 all-reduce.6
  122.5 58.5 all-reduce.8
  200.2 49.8 all-reduce.10
  259.0 59.2 all-reduce.12
where the time goes:
time: 338 us
  waiting for transfers between devices  169 us (50%)
  blocking collectives  102 us (30%)
  matrix products  36.3 us (11%)
  between operations  13.9 us (4%)
  other arithmetic  12.6 us (4%)
    psum x2, waiting for transfers between devices, local(): image = lax.psum(partial_rows, 'lm')  118 us
    psum x2, waiting for transfers between devices, local(): lax.psum(jnp.einsum('rl,rv->lv', build_tile, group_weighted, preferred_el...  50 us
    psum x1, blocking collectives, local(): totals = lax.psum(jnp.sum(weighted_full, axis=0), ('grp', 'lm'))  40.3 us
    psum x2, blocking collectives, local(): lax.psum((jnp.sum(image * image, axis=0), jnp.sum(weights[:, None] * imag...  19.7 us
    all_gather x1, blocking collectives, local(): lax.all_gather(weighted_full.astype(jnp.bfloat16), 'lm', axis=0, tiled=True)  17.3 us
    dot_general x2, matrix products, local(): jnp.dot(build_tile, side_b, preferred_element_type=jnp.float32)  14.1 us
    all_gather x1, blocking collectives, local(): lax.all_gather(row_weight.astype(jnp.bfloat16), 'lm', axis=0, tiled=True)  13.5 us
    psum x1, blocking collectives, local(): mean_sum, weight_sum = lax.psum((sums, jnp.sum(weights)), 'grp')  11.7 us
  transfers between devices with their start and end apart: 5, of which 4 were waited for; matrix products, arithmetic and copies ran while one was open for 1% of the time, Pallas kernels for 0%

commit v1 on v0

--- a/solution.py
+++ b/solution.py
@@ -58,7 +58,10 @@
         partial_rows = weights[:, None] * (
             jnp.dot(build_tile, side_b, preferred_element_type=jnp.float32) - shift[None, :]
         )
-        image = lax.psum(partial_rows, "lm")
+        size, image = (lax.axis_size("lm"), partial_rows)
+        for far in [1 << k for k in range(size.bit_length() - 1)]:
+            route = [(i, i ^ far) for i in range(size)]
+            image = image + lax.ppermute(image, "lm", route)
         square, column = lax.psum(
             (jnp.sum(image * image, axis=0), jnp.sum(weights[:, None] * image, axis=0)), "grp"
         )

time: 338 us -> 367 us (1.086)
  waiting for transfers between devices: 169 us -> 198 us
  starting transfers between devices: 0.17 us -> 7.26 us
    ppermute x0 -> x6, waiting for transfers between devices: none -> 144 us  [local(): image = image + lax.ppermute(image, 'lm', route)]
    psum x2 -> x0, waiting for transfers between devices: 118 us -> none  [local(): image = lax.psum(partial_rows, 'lm')]
    ppermute x0 -> x6, starting transfers between devices: none -> 7.18 us  [local(): image = image + lax.ppermute(image, 'lm', route)]
  transfers between devices with their start and end apart: 5 -> 9, of which waited for: 4 -> 8; matrix products, arithmetic and copies ran while one was open for 1% -> 1% of each run, Pallas kernels for 0% -> 0%
where the time goes in v1:
time: 367 us; the launch traced here: 366 us
  waiting for transfers between devices  198 us (54%)
  blocking collectives  100 us (27%)
  matrix products  34.1 us (9%)
  between operations  13.9 us (4%)
  other arithmetic  9.71 us (3%)
  starting transfers between devices  7.26 us (2%)
    ppermute x6, waiting for transfers between devices, local(): image = image + lax.ppermute(image, 'lm', route)  144 us
    psum x2, waiting for transfers between devices, local(): lax.psum(jnp.einsum('rl,rv->lv', build_tile, group_weighted, preferred_el...  52.2 us
    psum x1, blocking collectives, local(): totals = lax.psum(jnp.sum(weighted_full, axis=0), ('grp', 'lm'))  40.3 us
    psum x2, blocking collectives, local(): lax.psum((jnp.sum(image * image, axis=0), jnp.sum(weights[:, None] * imag...  17.7 us
    all_gather x1, blocking collectives, local(): lax.all_gather(weighted_full.astype(jnp.bfloat16), 'lm', axis=0, tiled=True)  17.3 us
    all_gather x1, blocking collectives, local(): lax.all_gather(row_weight.astype(jnp.bfloat16), 'lm', axis=0, tiled=True)  13.5 us
    dot_general x2, matrix products, local(): jnp.dot(build_tile, side_b, preferred_element_type=jnp.float32)  12.2 us
    psum x1, blocking collectives, local(): mean_sum, weight_sum = lax.psum((sums, jnp.sum(weights)), 'grp')  11.7 us
  transfers between devices with their start and end apart: 9, of which 8 were waited for; matrix products, arithmetic and copies ran while one was open for 1% of the time, Pallas kernels for 0%

profile of v1, /device:TPU:0, one launch (start us, length us, event | category | flops | bytes accessed | tf_op | source)
XLA Modules:
  0.0 366.2 jit_solution(5030852468052424257)
XLA Ops:
  6.5 1.1 fusion.8
  7.6 1.8 fusion.9
  9.5 0.7 convert_element_type.35
  10.2 13.5 %all-gather = bf16[8,1,256]{2,1,0:T(2,128)(2,1)S(1)} all-gather(bf16[1,1,256]{2,1,0:T(2,128)(2,1)S(1)} %reshape.21), channel_id=1, replica_groups=mesh['grp'=4,'lm'=8] {'lm'}, dimensions={0}, use_global_device_ids=true | all-gather | bytes 4608 | tf_op jit(solution)/shard_map/all_gather | solution.py:33
  24.3 2.1 fusion.1
  26.4 1.0 multiply_reduce_fusion.4
  27.4 17.3 %all_gather.11 = bf16[2048,128]{1,0:T(8,128)(2,1)S(1)} all-gather(bf16[256,128]{1,0:T(8,128)(2,1)S(1)} %get-tuple-element.17), channel_id=1, replica_groups=mesh['grp'=4,'lm'=8] {'lm'}, dimensions={0}, use_global_device_ids=true | all-gather | bytes 589824 | tf_op jit(solution)/shard_map/all_gather | solution.py:45
  44.7 1.0 all-gather.3.cloned.1.call-done
  45.7 7.8 %multiply_reduce_fusion = (f32[2048]{0:T(1024)S(1)}, bf16[2048,2048]{1,0:T(8,128)(2,1)S(1)}) fusion(f32[2048]{0:T(1024)S(1)} %bitcast.19, f32[]{:T(128)} %bitcast.16, bf16[2048,512]{1,0:T(8,128)(2,1)} %all-gather.3.cloned.1.call-done, bf16[2048,512]{1,0:T(8,128)(2,1)} %param.6, f32[2048]{0:T(1024)S(1)} %add_rsqrt_fusion), kind=kOutput, calls=%fused_computation | convolution fusion | flops 4314888192 | bytes 12607492 | tf_op jit(solution)/shard_map/rd,ld->rl/dot_general | solution.py:16
  53.5 3.2 copy-done
  56.7 3.4 fusion.14
  60.2 40.3 %psum.59 = f32[128]{0:T(128)S(1)} all-reduce(f32[128]{0:T(128)S(1)} %get-tuple-element.16), channel_id=1, replica_groups=mesh['grp'=4,'lm'=8] {'grp','lm'}, use_global_device_ids=true, to_apply=%region_8.0 | all-reduce | flops 128 | bytes 1024 | tf_op jit(solution)/shard_map/psum | solution.py:44
  101.0 11.7 %all-reduce.1 = (f32[2048]{0:T(1024)S(1)}, f32[]{:T(128)}) all-reduce(f32[2048]{0:T(1024)S(1)} %get-tuple-element.14, f32[]{:T(128)} %convert_reduce_fusion), channel_id=1, replica_groups=mesh['grp'=4,'lm'=8] {'grp'}, use_global_device_ids=true, to_apply=%region_4.0 | all-reduce | flops 2049 | bytes 16392 | tf_op jit(solution)/shard_map/psum | solution.py:40
  113.5 1.8 convolution_bitcast_fusion.1
  115.3 6.1 %fusion.4 = f32[2048,128]{1,0:T(8,128)S(1)} fusion(bf16[2048,2048]{1,0:T(8,128)(2,1)} %copy-done, f32[128]{0:T(128)S(1)} %convolution_bitcast_fusion.1, f32[2048]{0:T(1024)S(1)} %bitcast.20, f32[2048,128]{1,0:T(8,128)} %all-reduce.5.cloned.1.call-done, f32[128]{0:T(128)S(1)} %psum.59, f32[2048]{0:T(1024)S(1)} %broadcast_divide_fusion), kind=kOutput, calls=%fused_computation.10 | convolution fusion | flops 1075052544 | bytes 10503168 | tf_op jit(solution)/shard_map/dot_general | solution.py:59
  121.5 2.6 collective-permute-done
  124.2 1.2 collective-permute-start.1
  125.4 24.1 %collective-permute-done.1 = f32[2048,128]{1,0:T(8,128)S(1)} collective-permute-done((f32[2048,128]{1,0:T(8,128)S(1)}, f32[2048,128]{1,0:T(8,128)S(1)}, u32[]{:S(2)}, u32[]{:S(2)}) %collective-permute-start.1) | collective-permute-done | bytes 1048608 | tf_op jit(solution)/shard_map/ppermute | solution.py:64
  149.6 1.8 collective-permute-start.2
  151.4 45.9 %collective-permute-done.2 = f32[2048,128]{1,0:T(8,128)S(1)} collective-permute-done((f32[2048,128]{1,0:T(8,128)S(1)}, f32[2048,128]{1,0:T(8,128)S(1)}, u32[]{:S(2)}, u32[]{:S(2)}) %collective-permute-start.2) | collective-permute-done | bytes 1048608 | tf_op jit(solution)/shard_map/ppermute | solution.py:64
  197.7 8.8 %all-reduce = (f32[128]{0:T(128)S(1)}, f32[128]{0:T(128)S(1)}) all-reduce(f32[128]{0:T(128)S(1)} %get-tuple-element.6, f32[128]{0:T(128)S(1)} %get-tuple-element.5), channel_id=1, replica_groups=mesh['grp'=4,'lm'=8] {'grp'}, use_global_device_ids=true, to_apply=%region_10.0 | all-reduce | flops 256 | bytes 2048 | tf_op jit(solution)/shard_map/psum | solution.py:65
  206.5 7.1 %fusion.10 = f32[2048,128]{1,0:T(8,128)} fusion(bf16[2048,2048]{1,0:T(8,128)(2,1)} %copy-done, f32[2048,128]{1,0:T(8,128)S(1)} %get-tuple-element.13, f32[128]{0:T(128)S(1)} %get-tuple-element.19, f32[2048]{0:T(1024)S(1)} %bitcast.22), kind=kOutput, calls=%fused_computation.25 | convolution fusion | flops 1074528256 | bytes 10494464 | tf_op jit(solution)/shard_map/rl,rv->lv/dot_general | solution.py:49
  213.7 52.2 %all-reduce.7.cloned.1.call-done = f32[2048,128]{1,0:T(8,128)} async-done(((f32[2048,128]{1,0:T(8,128)}), f32[2048,128]{1,0:T(8,128)}) %all-reduce.7.cloned.1.call-update) | async-done | bytes 1048592 | tf_op jit(solution)/shard_map/psum | solution.py:48
  265.9 1.8 convolution_bitcast_fusion
  267.7 6.1 %fusion.3 = f32[2048,128]{1,0:T(8,128)S(1)} fusion(bf16[2048,2048]{1,0:T(8,128)(2,1)} %copy-done, f32[128]{0:T(128)S(1)} %convolution_bitcast_fusion, f32[2048]{0:T(1024)S(1)} %bitcast.23, f32[2048,128]{1,0:T(8,128)} %all-reduce.7.cloned.1.call-done, f32[128]{0:T(128)S(1)} %get-tuple-element.18, f32[2048]{0:T(1024)S(1)} %broadcast_divide_fusion), kind=kOutput, calls=%fused_computation.8 | convolution fusion | flops 1075052544 | bytes 10503168 | tf_op jit(solution)/shard_map/dot_general | solution.py:59
  273.9 2.6 collective-permute-done.3
  276.6 1.6 collective-permute-start.4
  278.2 23.7 %collective-permute-done.4 = f32[2048,128]{1,0:T(8,128)S(1)} collective-permute-done((f32[2048,128]{1,0:T(8,128)S(1)}, f32[2048,128]{1,0:T(8,128)S(1)}, u32[]{:S(2)}, u32[]{:S(2)}) %collective-permute-start.4) | collective-permute-done | bytes 1048608 | tf_op jit(solution)/shard_map/ppermute | solution.py:64
  302.0 2.5 collective-permute-start.5
  304.5 45.3 %collective-permute-done.5 = f32[2048,128]{1,0:T(8,128)S(1)} collective-permute-done((f32[2048,128]{1,0:T(8,128)S(1)}, f32[2048,128]{1,0:T(8,128)S(1)}, u32[]{:S(2)}, u32[]{:S(2)}) %collective-permute-start.5) | collective-permute-done | bytes 1048608 | tf_op jit(solution)/shard_map/ppermute | solution.py:64
  350.1 8.9 %psum.63 = f32[128]{0:T(128)S(1)} all-reduce(f32[128]{0:T(128)S(1)} %get-tuple-element.11), channel_id=1, replica_groups=mesh['grp'=4,'lm'=8] {'grp'}, use_global_device_ids=true, to_apply=%region_15.0 | all-reduce | flops 128 | bytes 1024 | tf_op jit(solution)/shard_map/psum | solution.py:65
  359.0 0.7 dynamic-slice_divide_fusion
  (24 shorter events, 2.7 us)
Async XLA Ops:
  6.5 39.1 %all-gather.3.cloned.1.call-start = ((), (), s32[]{:S(2)}) async-start(), calls=%async_computation | async-start | bytes 2359296 | tf_op jit(solution)/shard_map/all_gather | solution.py:32
  9.4 104.0 %all-reduce.5.cloned.1.call-start = ((), (), s32[]{:S(2)}) async-start(), calls=%async_computation.1 | async-start | bytes 2097152 | tf_op jit(solution)/shard_map/psum | solution.py:48
  53.5 3.2 copy-start
  60.1 205.7 %all-reduce.7.cloned.1.call-start = ((), (), s32[]{:S(2)}) async-start(), calls=%async_computation.2 | async-start | bytes 2097152 | tf_op jit(solution)/shard_map/psum | solution.py:48
  121.4 2.7 collective-permute-start
  124.2 25.3 %collective-permute-start.1 = (f32[2048,128]{1,0:T(8,128)S(1)}, f32[2048,128]{1,0:T(8,128)S(1)}, u32[]{:S(2)}, u32[]{:S(2)}) collective-permute-start(f32[2048,128]{1,0:T(8,128)S(1)} %add.69), channel_id=1, source_target_pairs={{0,2},{1,3},{2,0},{3,1},{4,6},{5,7},{6,4},{7,5},{8,10},{9,11},{10,... | collective-permute-start | bytes 3145736 | tf_op jit(solution)/shard_map/ppermute | solution.py:64
  149.6 47.8 %collective-permute-start.2 = (f32[2048,128]{1,0:T(8,128)S(1)}, f32[2048,128]{1,0:T(8,128)S(1)}, u32[]{:S(2)}, u32[]{:S(2)}) collective-permute-start(f32[2048,128]{1,0:T(8,128)S(1)} %add.70), channel_id=1, source_target_pairs={{0,4},{1,5},{2,6},{3,7},{4,0},{5,1},{6,2},{7,3},{8,12},{9,13},{10,... | collective-permute-start | bytes 3145736 | tf_op jit(solution)/shard_map/ppermute | solution.py:64
  273.8 2.7 collective-permute-start.3
  276.6 25.3 %collective-permute-start.4 = (f32[2048,128]{1,0:T(8,128)S(1)}, f32[2048,128]{1,0:T(8,128)S(1)}, u32[]{:S(2)}, u32[]{:S(2)}) collective-permute-start(f32[2048,128]{1,0:T(8,128)S(1)} %add.73), channel_id=1, source_target_pairs={{0,2},{1,3},{2,0},{3,1},{4,6},{5,7},{6,4},{7,5},{8,10},{9,11},{10,... | collective-permute-start | bytes 3145736 | tf_op jit(solution)/shard_map/ppermute | solution.py:64
  302.0 47.8 %collective-permute-start.5 = (f32[2048,128]{1,0:T(8,128)S(1)}, f32[2048,128]{1,0:T(8,128)S(1)}, u32[]{:S(2)}, u32[]{:S(2)}) collective-permute-start(f32[2048,128]{1,0:T(8,128)S(1)} %add.74), channel_id=1, source_target_pairs={{0,4},{1,5},{2,6},{3,7},{4,0},{5,1},{6,2},{7,3},{8,12},{9,13},{10,... | collective-permute-start | bytes 3145736 | tf_op jit(solution)/shard_map/ppermute | solution.py:64
Sparse Core Ops, SparseCore 0:
  9.6 36.0 all-gather.2
  60.2 52.8 all-reduce.4
  213.8 51.9 all-reduce.6
